TPU v7x, 32 devices: a whole 2x2x4 slice. The times are simulated.
32 devices in a mesh: slab: 8 (over y, x, core), grp: 4 (over z).
Axes of the slice: x: 2, y: 2, z: 4, core: 2. Of those that a mesh axis runs over, the one named last changes fastest.
Arguments:
- resid7: float32 [512, 4096], P(None, ('slab', 'grp')), may hold values from -6 to 6
- interp73: float32 [8, 4], replicated, may hold values from -2 to 2
- interp31: float32 [4, 2], replicated, may hold values from -4 to 4
- elem_ops: float32 [8, 8, 4096], P(None, None, 'slab'), as said below
- conn: int32 [8, 4096], P(None, 'slab'), may hold values from 0 to 1121, as said below
- faces: int32 [2, 8, 561], P(None, 'slab'), may hold values from 0 to 1121, as said below
Outputs:
- correction3: float32 [64, 4096], P(None, ('slab', 'grp'))
Inputs may be any that keep to these rules, and one draw needn't show every extreme that they name: `conn`: the 512 columns of a slab describe a block of 32 x 16 x 1 hexahedra stacked along the long direction; column e lists the corners of one element, the corner at offsets (i, j, k) along (long, second, first direction) in row 4 i + 2 j + k; the slab's nodes are numbered 0 to 1121 in some order and every one of them is a corner of some element. faces[0, s] lists the 561 nodes of slab s on its face toward slab s - 1, faces[1, s] those on its face toward slab s + 1, all distinct; faces[1, s, f] and faces[0, s + 1, f] are the same point of the mesh. `elem_ops`: each element's matrix is symmetric, and each diagonal entry is positive and larger than the sum of magnitudes of the other entries of its row.
All inputs are finite; a program needn't handle non-finite values.
Results may differ from a plain program's by a relative error of at most 0.0003.
Values sent between devices are 32-bit elements; how exact they have to be, the bound alone decides.
A program may use at most 64 MiB of HBM per device.

v0:
```python
import jax
import jax.numpy as jnp
from jax import lax
from jax.sharding import PartitionSpec as P

EX = 32
EY = 16
SWEEPS = 2
lam_low = 0.3
lam_high = 1.9


def extended(array, sides, width):
    for axis, dim in sides:
        count, length = (lax.axis_size(axis), array.shape[dim])
        up = [(i, (i + 1) % count) for i in range(count - 1)]
        down = [(j, i) for i, j in up]
        last = lax.slice_in_dim(array, length - width, length, axis=dim)
        first = lax.slice_in_dim(array, 0, width, axis=dim)
        before = lax.ppermute(last, axis, up)
        after = lax.ppermute(first, axis, down)
        array = jnp.concatenate([before, array, after], axis=dim)
    return array


def restrict_high(block, interp73):
    hi = lax.Precision.HIGHEST
    width = block.shape[1]
    cube = block.reshape(8, 8, 8, width)
    cube = jnp.einsum("kc,ijkm->ijcm", interp73, cube, precision=hi)
    cube = jnp.einsum("jb,ijcm->ibcm", interp73, cube, precision=hi)
    cube = jnp.einsum("ia,ibcm->abcm", interp73, cube, precision=hi)
    return cube.reshape(64, width)


def restrict_low(block, interp31):
    hi = lax.Precision.HIGHEST
    width = block.shape[1]
    cube = block.reshape(4, 4, 4, width)
    cube = jnp.einsum("kc,ijkm->ijcm", interp31, cube, precision=hi)
    cube = jnp.einsum("jb,ijcm->ibcm", interp31, cube, precision=hi)
    cube = jnp.einsum("ia,ibcm->abcm", interp31, cube, precision=hi)
    return cube.reshape(8, width)


def prolong(coarse, interp31):
    hi = lax.Precision.HIGHEST
    width = coarse.shape[1]
    cube = coarse.reshape(2, 2, 2, width)
    cube = jnp.einsum("ck,ijkm->ijcm", interp31, cube, precision=hi)
    cube = jnp.einsum("bj,ijcm->ibcm", interp31, cube, precision=hi)
    cube = jnp.einsum("ai,ibcm->abcm", interp31, cube, precision=hi)
    return cube.reshape(64, width)


def assemble(values, conn_ids, count):
    layers = values.shape[0]
    flat = values.reshape(layers, -1).T
    summed = jax.ops.segment_sum(flat, conn_ids.reshape(-1), num_segments=count)
    return summed.T


def element_term(operators, conn_ids, field):
    return jnp.einsum("pqe,qe->pe", operators, field[conn_ids], precision=lax.Precision.HIGHEST)


def share(nodes, faces):
    lower = faces[0, 0]
    upper = faces[1, 0]
    planes = jnp.stack([nodes[:, lower], nodes[:, upper]], axis=1)
    padded = extended(planes, (("slab", 1),), 1)
    return nodes.at[:, lower].add(padded[:, 0]).at[:, upper].add(padded[:, 3])


def local(resid7, interp73, interp31, elem_ops, conn, faces):
    own = resid7.shape[1]
    slab_elems = conn.shape[1]
    layers = slab_elems // (EX * EY)
    count = (EX + 1) * (EY + 1) * (layers + 1)
    start = lax.axis_index("grp") * own
    own_conn = lax.dynamic_slice_in_dim(conn, start, own, 1)
    middle_res = restrict_high(resid7, interp73)
    blocks = lax.all_gather(middle_res, "grp", axis=1, tiled=True)
    slab_res = restrict_low(blocks, interp31)
    pair = jnp.stack([slab_res, jnp.einsum("ppe->pe", elem_ops)])
    both_nodes = assemble(pair, conn, count)
    shared = share(both_nodes, faces)
    rhs = shared[0]
    diag = shared[1]
    theta = 0.5 * (lam_high + lam_low)
    delta = 0.5 * (lam_high - lam_low)
    sigma = theta / delta
    inverse = 1.0 / diag
    direction = inverse * rhs / theta
    solution = direction
    remain = rhs
    rho = 1.0 / sigma
    for sweep in range(SWEEPS):
        nodes = assemble(element_term(elem_ops, conn, direction)[None], conn, count)
        remain = remain - share(nodes, faces)[0]
        rho_new = 1.0 / (2.0 * sigma - rho)
        direction = rho_new * rho * direction + 2.0 * rho_new / delta * inverse * remain
        solution = solution + direction
        rho = rho_new
    return prolong(solution[own_conn], interp31)


def solution(mesh):
    in_specs = (
        P(None, ("slab", "grp")),
        P(),
        P(),
        P(None, None, "slab"),
        P(None, "slab"),
        P(None, "slab", None),
    )
    out_specs = P(None, ("slab", "grp"))
    return jax.shard_map(local, mesh=mesh, in_specs=in_specs, out_specs=out_specs, check_vma=False)
```

profile of v0, /device:TPU:12, one launch (start us, length us, event | category | flops | bytes accessed | tf_op | source)
XLA Modules:
  0.0 223.9 jit_solution(7532873134520829746)
XLA Ops:
  0.0 0.0 copy-start
  0.0 0.0 copy-start.4
  0.0 0.8 copy.70
  0.8 1.0 select_reduce_fusion
  1.8 0.0 copy-done
  1.8 1.0 convolution_bitcast_fusion
  2.8 0.0 copy-start.2
  2.8 0.9 convolution_bitcast_fusion.2
  3.8 0.9 convolution_bitcast_fusion.5
  4.7 13.9 %all_gather.3 = f32[64,512]{1,0:T(8,128)S(1)} all-gather(f32[64,128]{1,0:T(8,128)S(1)} %bitcast.100), channel_id=1, replica_groups=mesh['slab'=8,'grp'=4] {'grp'}, dimensions={1}, use_global_device_ids=true | all-gather | bytes 163840 | tf_op jit(solution)/shard_map/all_gather | solution.py:83
  18.6 1.0 convolution_bitcast_fusion.1
  19.7 0.9 convolution_bitcast_fusion.4
  20.6 0.9 convolution_bitcast_fusion.7
  21.6 0.7 copy.46
  22.2 0.0 copy-done.4
  22.3 22.5 %scatter_custom_fusion = f32[1122,2]{1,0:T(8,128)S(1)} fusion(s32[4096]{0:T(1024)S(1)} %bitcast.109, f32[4096,2]{1,0:T(8,128)S(1)} %copy.46, f32[]{:T(128)} %constant.13.clone.1), kind=kCustom, calls=%fused_computation.31 | custom fusion | flops 8192 | bytes 8980 | tf_op jit(solution)/shard_map/scatter-add | solution.py:59
  44.8 1.6 gather_fusion
  46.4 1.9 collective-permute-start
  48.3 1.6 gather_fusion.1
  49.9 4.5 %collective-permute-start.1 = (f32[2,1,561]{0,2,1:T(8,128)S(1)}, f32[2,1,561]{0,2,1:T(8,128)S(1)}, u32[]{:S(2)}, u32[]{:S(2)}) collective-permute-start(f32[2,1,561]{0,2,1:T(8,128)S(1)} %bitcast.115), channel_id=1, source_target_pairs={{4,0},{8,4},{12,8},{16,12},{20,16},{24,20},{28,24},{5,1},{9,5},{13... | collective-permute-start | bytes 13472 | tf_op jit(solution)/shard_map/ppermute | solution.py:21
  54.5 0.0 copy-done.2
  54.5 0.7 collective-permute-done
  55.3 6.4 %scatter_custom_fusion.1 = f32[2,1122]{0,1:T(8,128)S(1)} fusion(f32[2,1122]{0,1:T(8,128)S(1)} %bitcast.99, s32[561]{0:T(1024)S(1)} %get-tuple-element.6, f32[2,1,561]{0,2,1:T(8,128)S(1)} %collective-permute-done), kind=kCustom, calls=%fused_computation.29 | custom fusion | flops 1122 | bytes 299792 | tf_op jit(solution)/shard_map/scatter-add | solution.py:72
  61.7 0.0 collective-permute-done.1
  61.7 6.4 %scatter_custom_fusion.2 = f32[2,1122]{0,1:T(8,128)S(1)} fusion(f32[2,1122]{0,1:T(8,128)S(1)} %scatter_custom_fusion.1, s32[561]{0:T(1024)S(1)} %get-tuple-element.5, f32[2,1,561]{0,2,1:T(8,128)S(1)} %collective-permute-done.1), kind=kCustom, calls=%fused_computation.27 | custom fusion | flops 1122 | bytes 299792 | tf_op jit(solution)/shard_map/scatter-add | solution.py:72
  68.1 0.2 fusion.32
  68.3 0.2 copy.67
  68.5 0.2 copy.66
  68.8 0.1 multiply_reduce_fusion.2
  68.8 0.0 copy-start.1
  68.8 23.0 %gather_fusion.2 = f32[4096]{0:T(1024)S(1)} fusion(f32[1122]{0:T(1024)S(1)} %get-tuple-element.7, s32[4096]{0:T(1024)S(1)} %broadcast_clamp_fusion), kind=kCustom, calls=%fused_computation.2 | custom fusion | bytes 49152 | tf_op jit(solution)/shard_map/gather | solution.py:64
  91.9 0.0 copy-done.1
  92.0 26.4 %scatter_custom_fusion.3 = f32[1122]{0:T(1024)S(1)} fusion(s32[4096]{0:T(1024)S(1)} %bitcast.110, f32[4096]{0:T(1024)S(1)} %bitcast.113, f32[]{:T(128)} %constant.13.clone.1), kind=kCustom, calls=%fused_computation.62 | custom fusion | flops 4096 | bytes 4492 | tf_op jit(solution)/shard_map/scatter-add | solution.py:59
  118.4 3.6 %gather_fusion.3 = f32[561]{0:T(1024)S(1)} fusion(f32[1122]{0:T(1024)S(1)} %scatter_custom_fusion.3, s32[1024]{0:T(1024)S(1)} %get-tuple-element.12), kind=kCustom, calls=%fused_computation.3 | custom fusion | bytes 6732 | tf_op jit(solution)/shard_map/gather | solution.py:70
  122.0 2.1 collective-permute-start.2
  124.1 3.6 %gather_fusion.4 = f32[561]{0:T(1024)S(1)} fusion(f32[1122]{0:T(1024)S(1)} %scatter_custom_fusion.3, s32[1024]{0:T(1024)S(1)} %get-tuple-element.11), kind=kCustom, calls=%fused_computation.4 | custom fusion | bytes 6732 | tf_op jit(solution)/shard_map/gather | solution.py:70
  127.7 4.4 %collective-permute-start.3 = (f32[1,1,561]{2,1,0:T(1,128)S(1)}, f32[1,1,561]{2,1,0:T(1,128)S(1)}, u32[]{:S(2)}, u32[]{:S(2)}) collective-permute-start(f32[1,1,561]{2,1,0:T(1,128)S(1)} %stack.32), channel_id=1, source_target_pairs={{4,0},{8,4},{12,8},{16,12},{20,16},{24,20},{28,24},{5,1},{9,5},{13... | collective-permute-start | bytes 6740 | tf_op jit(solution)/shard_map/ppermute | solution.py:21
  132.0 0.0 collective-permute-done.2
  132.1 5.3 %scatter_fusion = f32[1122]{0:T(1024)S(1)} fusion(f32[1122]{0:T(1024)S(1)} %scatter_custom_fusion.3, s32[561]{0:T(1024)S(1)} %get-tuple-element.6, f32[561]{0:T(1024)S(1)} %reduce.5), kind=kCustom, calls=%fused_computation.13 | custom fusion | flops 561 | bytes 8976 | tf_op jit(solution)/shard_map/scatter-add | solution.py:72
  137.3 0.0 collective-permute-done.3
  137.4 5.2 %scatter_fusion.1 = f32[1122]{0:T(1024)S(1)} fusion(f32[1122]{0:T(1024)S(1)} %scatter_fusion, s32[561]{0:T(1024)S(1)} %get-tuple-element.5, f32[561]{0:T(1024)S(1)} %reduce.6), kind=kCustom, calls=%fused_computation.14 | custom fusion | flops 561 | bytes 8976 | tf_op jit(solution)/shard_map/scatter-add | solution.py:72
  142.6 23.0 %gather_fusion.5 = f32[4096]{0:T(1024)S(1)} fusion(f32[1122]{0:T(1024)S(1)} %add_reduce_fusion, s32[4096]{0:T(1024)S(1)} %broadcast_clamp_fusion), kind=kCustom, calls=%fused_computation.5 | custom fusion | bytes 49152 | tf_op jit(solution)/shard_map/gather | solution.py:64
  165.7 26.4 %scatter_custom_fusion.6 = f32[1122]{0:T(1024)S(1)} fusion(s32[4096]{0:T(1024)S(1)} %bitcast.111, f32[4096]{0:T(1024)S(1)} %bitcast.112, f32[]{:T(128)} %constant.13.clone.1), kind=kCustom, calls=%fused_computation.60 | custom fusion | flops 4096 | bytes 4492 | tf_op jit(solution)/shard_map/scatter-add | solution.py:59
  192.2 3.6 %gather_fusion.7 = f32[561]{0:T(1024)S(1)} fusion(f32[1122]{0:T(1024)S(1)} %scatter_custom_fusion.6, s32[1024]{0:T(1024)S(1)} %get-tuple-element.11), kind=kCustom, calls=%fused_computation.7 | custom fusion | bytes 6732 | tf_op jit(solution)/shard_map/gather | solution.py:70
  195.7 3.6 %gather_fusion.6 = f32[561]{0:T(1024)S(1)} fusion(f32[1122]{0:T(1024)S(1)} %scatter_custom_fusion.6, s32[1024]{0:T(1024)S(1)} %get-tuple-element.12), kind=kCustom, calls=%fused_computation.6 | custom fusion | bytes 6732 | tf_op jit(solution)/shard_map/gather | solution.py:70
  199.3 1.9 collective-permute-start.4
  201.2 4.5 %collective-permute-start.5 = (f32[1,1,561]{2,1,0:T(1,128)S(1)}, f32[1,1,561]{2,1,0:T(1,128)S(1)}, u32[]{:S(2)}, u32[]{:S(2)}) collective-permute-start(f32[1,1,561]{2,1,0:T(1,128)S(1)} %stack.34), channel_id=1, source_target_pairs={{4,0},{8,4},{12,8},{16,12},{20,16},{24,20},{28,24},{5,1},{9,5},{13... | collective-permute-start | bytes 6740 | tf_op jit(solution)/shard_map/ppermute | solution.py:21
  205.8 0.0 collective-permute-done.4
  205.8 5.3 %scatter_fusion.2 = f32[1122]{0:T(1024)S(1)} fusion(f32[1122]{0:T(1024)S(1)} %scatter_custom_fusion.6, s32[561]{0:T(1024)S(1)} %get-tuple-element.6, f32[561]{0:T(1024)S(1)} %reduce.8), kind=kCustom, calls=%fused_computation.16 | custom fusion | flops 561 | bytes 8976 | tf_op jit(solution)/shard_map/scatter-add | solution.py:72
  211.1 0.0 collective-permute-done.5
  211.2 5.2 %scatter_fusion.3 = f32[1122]{0:T(1024)S(1)} fusion(f32[1122]{0:T(1024)S(1)} %scatter_fusion.2, s32[561]{0:T(1024)S(1)} %get-tuple-element.5, f32[561]{0:T(1024)S(1)} %reduce.9), kind=kCustom, calls=%fused_computation.17 | custom fusion | flops 561 | bytes 8976 | tf_op jit(solution)/shard_map/scatter-add | solution.py:72
  216.4 0.0 copy-start.3
  216.4 6.2 %gather_fusion.8 = f32[1024]{0:T(1024)S(1)} fusion(f32[1122]{0:T(1024)S(1)} %add_add_fusion, s32[1024]{0:T(1024)S(1)} %fusion.16), kind=kCustom, calls=%fused_computation.8 | custom fusion | bytes 12288 | tf_op jit(solution)/shard_map/gather | solution.py:105
  222.6 0.0 copy-done.3
  222.6 0.2 convolution_bitcast_fusion.8
  222.8 0.2 convolution_bitcast_fusion.6
  223.0 0.3 convolution_bitcast_fusion.3
  223.3 0.6 copy.51
  (30 shorter events, 0.4 us)
Async XLA Ops:
  0.0 1.8 copy-start
  0.0 22.2 %copy-start.4 = (s32[2,1,561]{2,1,0:T(1,128)S(1)}, s32[2,1,561]{2,1,0:T(1,128)}, u32[]{:S(2)}) copy-start(s32[2,1,561]{2,1,0:T(1,128)} %param.11) | copy-start | bytes 13468
  2.8 51.7 %copy-start.2 = (s32[8,512]{1,0:T(8,128)S(1)}, s32[8,512]{1,0:T(8,128)}, u32[]{:S(2)}) copy-start(s32[8,512]{1,0:T(8,128)} %param.10) | copy-start | bytes 49156
  46.4 8.9 %collective-permute-start = (f32[2,1,561]{0,2,1:T(8,128)S(1)}, f32[2,1,561]{0,2,1:T(8,128)S(1)}, u32[]{:S(2)}, u32[]{:S(2)}) collective-permute-start(f32[2,1,561]{0,2,1:T(8,128)S(1)} %bitcast.116), channel_id=1, source_target_pairs={{0,4},{4,8},{8,12},{12,16},{16,20},{20,24},{24,28},{1,5},{5,9},{9,... | collective-permute-start | bytes 13472 | tf_op jit(solution)/shard_map/ppermute | solution.py:20
  49.9 11.7 %collective-permute-start.1 = (f32[2,1,561]{0,2,1:T(8,128)S(1)}, f32[2,1,561]{0,2,1:T(8,128)S(1)}, u32[]{:S(2)}, u32[]{:S(2)}) collective-permute-start(f32[2,1,561]{0,2,1:T(8,128)S(1)} %bitcast.115), channel_id=1, source_target_pairs={{4,0},{8,4},{12,8},{16,12},{20,16},{24,20},{28,24},{5,1},{9,5},{13... | collective-permute-start | bytes 13472 | tf_op jit(solution)/shard_map/ppermute | solution.py:21
  68.8 23.1 %copy-start.1 = (f32[8,8,512]{2,1,0:T(8,128)S(1)}, f32[8,8,512]{2,1,0:T(8,128)}, u32[]{:S(2)}) copy-start(f32[8,8,512]{2,1,0:T(8,128)} %param.9) | copy-start | bytes 393220
  122.0 10.1 %collective-permute-start.2 = (f32[1,1,561]{2,1,0:T(1,128)S(1)}, f32[1,1,561]{2,1,0:T(1,128)S(1)}, u32[]{:S(2)}, u32[]{:S(2)}) collective-permute-start(f32[1,1,561]{2,1,0:T(1,128)S(1)} %stack.31), channel_id=1, source_target_pairs={{0,4},{4,8},{8,12},{12,16},{16,20},{20,24},{24,28},{1,5},{5,9},{9,... | collective-permute-start | bytes 6740 | tf_op jit(solution)/shard_map/ppermute | solution.py:20
  127.7 9.7 %collective-permute-start.3 = (f32[1,1,561]{2,1,0:T(1,128)S(1)}, f32[1,1,561]{2,1,0:T(1,128)S(1)}, u32[]{:S(2)}, u32[]{:S(2)}) collective-permute-start(f32[1,1,561]{2,1,0:T(1,128)S(1)} %stack.32), channel_id=1, source_target_pairs={{4,0},{8,4},{12,8},{16,12},{20,16},{24,20},{28,24},{5,1},{9,5},{13... | collective-permute-start | bytes 6740 | tf_op jit(solution)/shard_map/ppermute | solution.py:21
  199.3 6.5 %collective-permute-start.4 = (f32[1,1,561]{2,1,0:T(1,128)S(1)}, f32[1,1,561]{2,1,0:T(1,128)S(1)}, u32[]{:S(2)}, u32[]{:S(2)}) collective-permute-start(f32[1,1,561]{2,1,0:T(1,128)S(1)} %stack.33), channel_id=1, source_target_pairs={{0,4},{4,8},{8,12},{12,16},{16,20},{20,24},{24,28},{1,5},{5,9},{9,... | collective-permute-start | bytes 6740 | tf_op jit(solution)/shard_map/ppermute | solution.py:20
  201.2 9.9 %collective-permute-start.5 = (f32[1,1,561]{2,1,0:T(1,128)S(1)}, f32[1,1,561]{2,1,0:T(1,128)S(1)}, u32[]{:S(2)}, u32[]{:S(2)}) collective-permute-start(f32[1,1,561]{2,1,0:T(1,128)S(1)} %stack.34), channel_id=1, source_target_pairs={{4,0},{8,4},{12,8},{16,12},{20,16},{24,20},{28,24},{5,1},{9,5},{13... | collective-permute-start | bytes 6740 | tf_op jit(solution)/shard_map/ppermute | solution.py:21
  216.4 6.2 %copy-start.3 = (f32[4,2]{0,1:T(2,128)S(1)}, f32[4,2]{0,1:T(2,128)}, u32[]{:S(2)}) copy-start(f32[4,2]{0,1:T(2,128)} %param.8) | copy-start | bytes 100
where the time goes:
time: 224 us
  other arithmetic  110 us (49%)
  local copies, waits for them, and re-layouts  72.5 us (32%)
  starting transfers between devices  19.4 us (9%)
  blocking collectives  13.9 us (6%)
  matrix products  6.36 us (3%)
    scatter-add x3, other arithmetic, assemble(): summed = jax.ops.segment_sum(flat, conn_ids.reshape(-1), num_segments=count)  75.3 us
    gather x4, local copies, waits for them, and re-layouts, element_term(): field[conn_ids]  46.1 us
    scatter-add x6, other arithmetic, share(): return nodes.at[:, lower].add(padded[:, 0]).at[:, upper].add(padded[:, 3])  33.7 us
    gather x6, local copies, waits for them, and re-layouts, share(): planes = jnp.stack([nodes[:, lower], nodes[:, upper]], axis=1)  17.5 us
    all_gather x1, blocking collectives, local(): blocks = lax.all_gather(middle_res, 'grp', axis=1, tiled=True)  13.9 us
    ppermute x3, starting transfers between devices, extended(): after = lax.ppermute(first, axis, down)  13.4 us
    gather x1, local copies, waits for them, and re-layouts, local(): return prolong(solution[own_conn], interp31)  6.15 us
    ppermute x3, starting transfers between devices, extended(): before = lax.ppermute(last, axis, up)  5.94 us
  transfers between devices with their start and end apart: 6, of which 1 were waited for; matrix products, arithmetic and copies ran while one was open for 10% of the time, Pallas kernels for 0%

commit v1 on v0

--- a/solution.py
+++ b/solution.py
@@ -80,7 +80,24 @@
     start = lax.axis_index("grp") * own
     own_conn = lax.dynamic_slice_in_dim(conn, start, own, 1)
     middle_res = restrict_high(resid7, interp73)
-    blocks = lax.all_gather(middle_res, "grp", axis=1, tiled=True)
+    opened = jax.lax.psum(1, axis_name="grp")
+    block_last = jax.lax.axis_index("grp")
+    state_next, w_next, carry = (opened, block_last, middle_res.shape[1])
+    plain, later = (middle_res, 1)
+    while later < state_next:
+        plain = jnp.concatenate(
+            [
+                plain,
+                jax.lax.ppermute(
+                    plain,
+                    axis_name="grp",
+                    perm=[(c, (c - later) % state_next) for c in range(state_next)],
+                ),
+            ],
+            1,
+        )
+        later = 2 * later
+    blocks = jnp.roll(plain, w_next * carry, 1)
     slab_res = restrict_low(blocks, interp31)
     pair = jnp.stack([slab_res, jnp.einsum("ppe->pe", elem_ops)])
     both_nodes = assemble(pair, conn, count)

time: 224 us -> 221 us (0.987); the launches traced: 224 us -> 219 us
  blocking collectives: 13.9 us -> 0 us
  starting transfers between devices: 19.4 us -> 24.3 us
  other arithmetic: 110 us -> 113 us
  waiting for transfers between devices: 0.76 us -> 3.26 us
    all_gather x1 -> x0, blocking collectives: 13.9 us -> none  [local(): blocks = lax.all_gather(middle_res, 'grp', axis=1, tiled=True)]
    ppermute x0 -> x2, starting transfers between devices: none -> 4.89 us  [local(): jax.lax.ppermute(plain, axis_name='grp', perm=[(c, (c - later) % state_ne...]
    ppermute x0 -> x2, waiting for transfers between devices: none -> 2.46 us  [local(): jax.lax.ppermute(plain, axis_name='grp', perm=[(c, (c - later) % state_ne...]
  transfers between devices with their start and end apart: 6 -> 8, of which waited for: 1 -> 3; matrix products, arithmetic and copies ran while one was open for 10% -> 12% of each run, Pallas kernels for 0% -> 0%
where the time goes in v1:
time: 221 us; the launch traced here: 219 us
  other arithmetic  113 us (51%)
  local copies, waits for them, and re-layouts  73.5 us (33%)
  starting transfers between devices  24.3 us (11%)
  matrix products  4.33 us (2%)
  waiting for transfers between devices  3.26 us (1%)
    scatter-add x3, other arithmetic, assemble(): summed = jax.ops.segment_sum(flat, conn_ids.reshape(-1), num_segments=count)  75.5 us
    gather x4, local copies, waits for them, and re-layouts, element_term(): field[conn_ids]  46.1 us
    scatter-add x6, other arithmetic, share(): return nodes.at[:, lower].add(padded[:, 0]).at[:, upper].add(padded[:, 3])  33.7 us
    gather x6, local copies, waits for them, and re-layouts, share(): planes = jnp.stack([nodes[:, lower], nodes[:, upper]], axis=1)  17.5 us
    ppermute x3, starting transfers between devices, extended(): after = lax.ppermute(first, axis, down)  13.6 us
    gather x1, local copies, waits for them, and re-layouts, local(): return prolong(solution[own_conn], interp31)  6.15 us
    ppermute x3, starting transfers between devices, extended(): before = lax.ppermute(last, axis, up)  5.76 us
    ppermute x2, starting transfers between devices, local(): jax.lax.ppermute(plain, axis_name='grp', perm=[(c, (c - later) % state_ne...  4.89 us
  transfers between devices with their start and end apart: 8, of which 3 were waited for; matrix products, arithmetic and copies ran while one was open for 12% of the time, Pallas kernels for 0%

profile of v1, /device:TPU:12, one launch (start us, length us, event | category | flops | bytes accessed | tf_op | source)
XLA Modules:
  0.0 218.6 jit_solution(14681502068480602413)
XLA Ops:
  0.0 0.0 copy-start
  0.0 0.9 copy-done
  1.0 0.0 copy-start.2
  1.0 1.0 convolution_bitcast_fusion
  2.0 0.9 convolution_bitcast_fusion.2
  2.9 0.9 convolution_bitcast_fusion.5
  3.8 0.5 collective-permute-start
  4.4 0.7 fusion.22
  5.1 0.7 fusion.10
  5.8 1.0 select_reduce_fusion
  6.9 0.7 copy.70
  7.6 0.2 collective-permute-done
  7.8 4.4 %collective-permute-start.1 = (f32[64,256]{1,0:T(8,128)S(1)}, f32[64,256]{1,0:T(8,128)S(1)}, u32[]{:S(2)}, u32[]{:S(2)}) collective-permute-start(f32[64,256]{1,0:T(8,128)S(1)} %pad_maximum_fusion), channel_id=1, source_target_pairs={{0,2},{1,3},{2,0},{3,1},{4,6},{5,7},{6,4},{7,5},{8,10},{9,11},{10,... | collective-permute-start | bytes 196616 | tf_op jit(solution)/shard_map/ppermute | solution.py:91
  12.2 2.2 %collective-permute-done.1 = f32[64,256]{1,0:T(8,128)S(1)} collective-permute-done((f32[64,256]{1,0:T(8,128)S(1)}, f32[64,256]{1,0:T(8,128)S(1)}, u32[]{:S(2)}, u32[]{:S(2)}) %collective-permute-start.1) | collective-permute-done | bytes 65568 | tf_op jit(solution)/shard_map/ppermute | solution.py:91
  14.6 0.0 copy-done.2
  14.6 0.3 convolution_bitcast_fusion.1
  14.9 0.3 convolution_bitcast_fusion.4
  15.2 0.2 convolution_bitcast_fusion.7
  15.5 0.7 copy.46
  16.1 22.5 %scatter_custom_fusion = f32[1122,2]{1,0:T(8,128)S(1)} fusion(s32[4096]{0:T(1024)S(1)} %bitcast.112, f32[4096,2]{1,0:T(8,128)S(1)} %copy.46, f32[]{:T(128)} %constant.17.clone.1), kind=kCustom, calls=%fused_computation.31 | custom fusion | flops 8192 | bytes 8980 | tf_op jit(solution)/shard_map/scatter-add | solution.py:59
  38.6 1.6 gather_fusion
  40.3 1.9 collective-permute-start.2
  42.2 1.6 gather_fusion.1
  43.8 4.5 %collective-permute-start.3 = (f32[2,1,561]{0,2,1:T(8,128)S(1)}, f32[2,1,561]{0,2,1:T(8,128)S(1)}, u32[]{:S(2)}, u32[]{:S(2)}) collective-permute-start(f32[2,1,561]{0,2,1:T(8,128)S(1)} %bitcast.118), channel_id=1, source_target_pairs={{4,0},{8,4},{12,8},{16,12},{20,16},{24,20},{28,24},{5,1},{9,5},{13... | collective-permute-start | bytes 13472 | tf_op jit(solution)/shard_map/ppermute | solution.py:21
  48.4 0.8 collective-permute-done.2
  49.2 6.4 %scatter_custom_fusion.1 = f32[2,1122]{0,1:T(8,128)S(1)} fusion(f32[2,1122]{0,1:T(8,128)S(1)} %bitcast.99, s32[561]{0:T(1024)S(1)} %get-tuple-element.6, f32[2,1,561]{0,2,1:T(8,128)S(1)} %collective-permute-done.2), kind=kCustom, calls=%fused_computation.29 | custom fusion | flops 1122 | bytes 299792 | tf_op jit(solution)/shard_map/scatter-add | solution.py:72
  55.6 0.0 collective-permute-done.3
  55.6 6.4 %scatter_custom_fusion.2 = f32[2,1122]{0,1:T(8,128)S(1)} fusion(f32[2,1122]{0,1:T(8,128)S(1)} %scatter_custom_fusion.1, s32[561]{0:T(1024)S(1)} %get-tuple-element.5, f32[2,1,561]{0,2,1:T(8,128)S(1)} %collective-permute-done.3), kind=kCustom, calls=%fused_computation.27 | custom fusion | flops 1122 | bytes 299792 | tf_op jit(solution)/shard_map/scatter-add | solution.py:72
  62.0 0.2 fusion.32
  62.2 0.2 copy.66
  62.4 0.2 copy.67
  62.6 0.1 multiply_reduce_fusion.2
  62.7 0.0 copy-start.1
  62.7 23.0 %gather_fusion.2 = f32[4096]{0:T(1024)S(1)} fusion(f32[1122]{0:T(1024)S(1)} %get-tuple-element.7, s32[4096]{0:T(1024)S(1)} %broadcast_clamp_fusion), kind=kCustom, calls=%fused_computation.2 | custom fusion | bytes 49152 | tf_op jit(solution)/shard_map/gather | solution.py:64
  85.7 0.0 copy-done.1
  85.8 26.6 %scatter_custom_fusion.3 = f32[1122]{0:T(1024)S(1)} fusion(s32[4096]{0:T(1024)S(1)} %bitcast.113, f32[4096]{0:T(1024)S(1)} %bitcast.116, f32[]{:T(128)} %constant.17.clone.1), kind=kCustom, calls=%fused_computation.69 | custom fusion | flops 4096 | bytes 4492 | tf_op jit(solution)/shard_map/scatter-add | solution.py:59
  112.4 3.6 %gather_fusion.3 = f32[561]{0:T(1024)S(1)} fusion(f32[1122]{0:T(1024)S(1)} %scatter_custom_fusion.3, s32[1024]{0:T(1024)S(1)} %get-tuple-element.12), kind=kCustom, calls=%fused_computation.3 | custom fusion | bytes 6732 | tf_op jit(solution)/shard_map/gather | solution.py:70
  116.0 1.9 collective-permute-start.4
  117.9 3.6 %gather_fusion.4 = f32[561]{0:T(1024)S(1)} fusion(f32[1122]{0:T(1024)S(1)} %scatter_custom_fusion.3, s32[1024]{0:T(1024)S(1)} %get-tuple-element.11), kind=kCustom, calls=%fused_computation.4 | custom fusion | bytes 6732 | tf_op jit(solution)/shard_map/gather | solution.py:70
  121.5 4.5 %collective-permute-start.5 = (f32[1,1,561]{2,1,0:T(1,128)S(1)}, f32[1,1,561]{2,1,0:T(1,128)S(1)}, u32[]{:S(2)}, u32[]{:S(2)}) collective-permute-start(f32[1,1,561]{2,1,0:T(1,128)S(1)} %stack.32), channel_id=1, source_target_pairs={{4,0},{8,4},{12,8},{16,12},{20,16},{24,20},{28,24},{5,1},{9,5},{13... | collective-permute-start | bytes 6740 | tf_op jit(solution)/shard_map/ppermute | solution.py:21
  126.1 0.0 collective-permute-done.4
  126.1 5.3 %scatter_fusion = f32[1122]{0:T(1024)S(1)} fusion(f32[1122]{0:T(1024)S(1)} %scatter_custom_fusion.3, s32[561]{0:T(1024)S(1)} %get-tuple-element.6, f32[561]{0:T(1024)S(1)} %reduce.5), kind=kCustom, calls=%fused_computation.13 | custom fusion | flops 561 | bytes 8976 | tf_op jit(solution)/shard_map/scatter-add | solution.py:72
  131.4 0.0 collective-permute-done.5
  131.4 5.2 %scatter_fusion.1 = f32[1122]{0:T(1024)S(1)} fusion(f32[1122]{0:T(1024)S(1)} %scatter_fusion, s32[561]{0:T(1024)S(1)} %get-tuple-element.5, f32[561]{0:T(1024)S(1)} %reduce.6), kind=kCustom, calls=%fused_computation.14 | custom fusion | flops 561 | bytes 8976 | tf_op jit(solution)/shard_map/scatter-add | solution.py:72
  136.6 23.0 %gather_fusion.5 = f32[4096]{0:T(1024)S(1)} fusion(f32[1122]{0:T(1024)S(1)} %add_reduce_fusion, s32[4096]{0:T(1024)S(1)} %broadcast_clamp_fusion), kind=kCustom, calls=%fused_computation.5 | custom fusion | bytes 49152 | tf_op jit(solution)/shard_map/gather | solution.py:64
  159.8 26.4 %scatter_custom_fusion.6 = f32[1122]{0:T(1024)S(1)} fusion(s32[4096]{0:T(1024)S(1)} %bitcast.114, f32[4096]{0:T(1024)S(1)} %bitcast.115, f32[]{:T(128)} %constant.17.clone.1), kind=kCustom, calls=%fused_computation.67 | custom fusion | flops 4096 | bytes 4492 | tf_op jit(solution)/shard_map/scatter-add | solution.py:59
  186.2 3.6 %gather_fusion.6 = f32[561]{0:T(1024)S(1)} fusion(f32[1122]{0:T(1024)S(1)} %scatter_custom_fusion.6, s32[1024]{0:T(1024)S(1)} %get-tuple-element.12), kind=kCustom, calls=%fused_computation.6 | custom fusion | bytes 6732 | tf_op jit(solution)/shard_map/gather | solution.py:70
  189.8 3.6 %gather_fusion.7 = f32[561]{0:T(1024)S(1)} fusion(f32[1122]{0:T(1024)S(1)} %scatter_custom_fusion.6, s32[1024]{0:T(1024)S(1)} %get-tuple-element.11), kind=kCustom, calls=%fused_computation.7 | custom fusion | bytes 6732 | tf_op jit(solution)/shard_map/gather | solution.py:70
  193.3 1.9 collective-permute-start.6
  195.3 4.5 %collective-permute-start.7 = (f32[1,1,561]{2,1,0:T(1,128)S(1)}, f32[1,1,561]{2,1,0:T(1,128)S(1)}, u32[]{:S(2)}, u32[]{:S(2)}) collective-permute-start(f32[1,1,561]{2,1,0:T(1,128)S(1)} %stack.34), channel_id=1, source_target_pairs={{4,0},{8,4},{12,8},{16,12},{20,16},{24,20},{28,24},{5,1},{9,5},{13... | collective-permute-start | bytes 6740 | tf_op jit(solution)/shard_map/ppermute | solution.py:21
  199.8 0.7 fusion.16
  200.5 0.0 collective-permute-done.6
  200.6 5.3 %scatter_fusion.2 = f32[1122]{0:T(1024)S(1)} fusion(f32[1122]{0:T(1024)S(1)} %scatter_custom_fusion.6, s32[561]{0:T(1024)S(1)} %get-tuple-element.6, f32[561]{0:T(1024)S(1)} %reduce.8), kind=kCustom, calls=%fused_computation.16 | custom fusion | flops 561 | bytes 8976 | tf_op jit(solution)/shard_map/scatter-add | solution.py:72
  205.8 0.0 collective-permute-done.7
  205.9 5.2 %scatter_fusion.3 = f32[1122]{0:T(1024)S(1)} fusion(f32[1122]{0:T(1024)S(1)} %scatter_fusion.2, s32[561]{0:T(1024)S(1)} %get-tuple-element.5, f32[561]{0:T(1024)S(1)} %reduce.9), kind=kCustom, calls=%fused_computation.17 | custom fusion | flops 561 | bytes 8976 | tf_op jit(solution)/shard_map/scatter-add | solution.py:72
  211.1 6.2 %gather_fusion.8 = f32[1024]{0:T(1024)S(1)} fusion(f32[1122]{0:T(1024)S(1)} %add_add_fusion, s32[1024]{0:T(1024)S(1)} %fusion.16), kind=kCustom, calls=%fused_computation.8 | custom fusion | bytes 12288 | tf_op jit(solution)/shard_map/gather | solution.py:122
  217.3 0.2 convolution_bitcast_fusion.8
  217.5 0.2 convolution_bitcast_fusion.6
  217.7 0.3 convolution_bitcast_fusion.3
  218.0 0.6 copy.51
  (35 shorter events, 0.5 us)
Async XLA Ops:
  0.0 1.0 copy-start
  1.0 13.6 %copy-start.2 = (f32[4,2]{0,1:T(2,128)S(1)}, f32[4,2]{0,1:T(2,128)}, u32[]{:S(2)}) copy-start(f32[4,2]{0,1:T(2,128)} %param.8) | copy-start | bytes 100
  3.8 4.0 %collective-permute-start = (f32[64,128]{1,0:T(8,128)S(1)}, f32[64,128]{1,0:T(8,128)S(1)}, u32[]{:S(2)}, u32[]{:S(2)}) collective-permute-start(f32[64,128]{1,0:T(8,128)S(1)} %bitcast.100), channel_id=1, source_target_pairs={{0,3},{1,0},{2,1},{3,2},{4,7},{5,4},{6,5},{7,6},{8,11},{9,8},{10,9... | collective-permute-start | bytes 98312 | tf_op jit(solution)/shard_map/ppermute | solution.py:91
  7.8 6.6 %collective-permute-start.1 = (f32[64,256]{1,0:T(8,128)S(1)}, f32[64,256]{1,0:T(8,128)S(1)}, u32[]{:S(2)}, u32[]{:S(2)}) collective-permute-start(f32[64,256]{1,0:T(8,128)S(1)} %pad_maximum_fusion), channel_id=1, source_target_pairs={{0,2},{1,3},{2,0},{3,1},{4,6},{5,7},{6,4},{7,5},{8,10},{9,11},{10,... | collective-permute-start | bytes 196616 | tf_op jit(solution)/shard_map/ppermute | solution.py:91
  40.3 8.9 %collective-permute-start.2 = (f32[2,1,561]{0,2,1:T(8,128)S(1)}, f32[2,1,561]{0,2,1:T(8,128)S(1)}, u32[]{:S(2)}, u32[]{:S(2)}) collective-permute-start(f32[2,1,561]{0,2,1:T(8,128)S(1)} %bitcast.119), channel_id=1, source_target_pairs={{0,4},{4,8},{8,12},{12,16},{16,20},{20,24},{24,28},{1,5},{5,9},{9,... | collective-permute-start | bytes 13472 | tf_op jit(solution)/shard_map/ppermute | solution.py:20
  43.8 11.7 %collective-permute-start.3 = (f32[2,1,561]{0,2,1:T(8,128)S(1)}, f32[2,1,561]{0,2,1:T(8,128)S(1)}, u32[]{:S(2)}, u32[]{:S(2)}) collective-permute-start(f32[2,1,561]{0,2,1:T(8,128)S(1)} %bitcast.118), channel_id=1, source_target_pairs={{4,0},{8,4},{12,8},{16,12},{20,16},{24,20},{28,24},{5,1},{9,5},{13... | collective-permute-start | bytes 13472 | tf_op jit(solution)/shard_map/ppermute | solution.py:21
  62.7 23.1 %copy-start.1 = (f32[8,8,512]{2,1,0:T(8,128)S(1)}, f32[8,8,512]{2,1,0:T(8,128)}, u32[]{:S(2)}) copy-start(f32[8,8,512]{2,1,0:T(8,128)} %param.9) | copy-start | bytes 393220
  116.0 10.1 %collective-permute-start.4 = (f32[1,1,561]{2,1,0:T(1,128)S(1)}, f32[1,1,561]{2,1,0:T(1,128)S(1)}, u32[]{:S(2)}, u32[]{:S(2)}) collective-permute-start(f32[1,1,561]{2,1,0:T(1,128)S(1)} %stack.31), channel_id=1, source_target_pairs={{0,4},{4,8},{8,12},{12,16},{16,20},{20,24},{24,28},{1,5},{5,9},{9,... | collective-permute-start | bytes 6740 | tf_op jit(solution)/shard_map/ppermute | solution.py:20
  121.5 9.9 %collective-permute-start.5 = (f32[1,1,561]{2,1,0:T(1,128)S(1)}, f32[1,1,561]{2,1,0:T(1,128)S(1)}, u32[]{:S(2)}, u32[]{:S(2)}) collective-permute-start(f32[1,1,561]{2,1,0:T(1,128)S(1)} %stack.32), channel_id=1, source_target_pairs={{4,0},{8,4},{12,8},{16,12},{20,16},{24,20},{28,24},{5,1},{9,5},{13... | collective-permute-start | bytes 6740 | tf_op jit(solution)/shard_map/ppermute | solution.py:21
  193.3 7.2 %collective-permute-start.6 = (f32[1,1,561]{2,1,0:T(1,128)S(1)}, f32[1,1,561]{2,1,0:T(1,128)S(1)}, u32[]{:S(2)}, u32[]{:S(2)}) collective-permute-start(f32[1,1,561]{2,1,0:T(1,128)S(1)} %stack.33), channel_id=1, source_target_pairs={{0,4},{4,8},{8,12},{12,16},{16,20},{20,24},{24,28},{1,5},{5,9},{9,... | collective-permute-start | bytes 6740 | tf_op jit(solution)/shard_map/ppermute | solution.py:20
  195.3 10.5 %collective-permute-start.7 = (f32[1,1,561]{2,1,0:T(1,128)S(1)}, f32[1,1,561]{2,1,0:T(1,128)S(1)}, u32[]{:S(2)}, u32[]{:S(2)}) collective-permute-start(f32[1,1,561]{2,1,0:T(1,128)S(1)} %stack.34), channel_id=1, source_target_pairs={{4,0},{8,4},{12,8},{16,12},{20,16},{24,20},{28,24},{5,1},{9,5},{13... | collective-permute-start | bytes 6740 | tf_op jit(solution)/shard_map/ppermute | solution.py:21
